TPU v7x, 32 devices: a whole 2x2x4 slice. The times are simulated.
32 devices in a mesh: wide: 8 (over y, x, core), narrow: 4 (over z).
Axes of the slice: x: 2, y: 2, z: 4, core: 2. Of those that a mesh axis runs over, the one named last changes fastest.
Arguments:
- amplitudes: float32 [2, 8, 8, 4, 128, 128], P(None, None, 'wide', 'narrow'), may hold values from -6 to 6
- gates: float32 [3, 2, 2, 128, 128], replicated, may hold values from -0.375 to 0.375
Outputs:
- final_state: float32 [2, 8, 8, 4, 128, 128], P(None, None, 'wide', 'narrow')
All inputs are finite; a program needn't handle non-finite values.
Results may differ from a plain program's by a relative error of at most 0.0001.
Values sent between devices are 32-bit elements; how exact they have to be, the bound alone decides.
A program may use at most 64 MiB of HBM per device.

v0:
```python
import functools

import jax
import jax.numpy as jnp
from jax import lax
from jax.experimental import pallas as pl
from jax.experimental.pallas import tpu as pltpu
from jax.sharding import PartitionSpec as P

precise = lax.Precision.HIGHEST
MESH = pl.DeviceIdType.MESH
F32 = jnp.float32
BF16 = jnp.bfloat16
EARLY_AT = 4
TAIL = 1


def blocks(matrix):
    return jnp.stack([jnp.stack([matrix[0], -matrix[1]]), jnp.stack([matrix[1], matrix[0]])])


def on_rows(vector, matrix):
    return jnp.einsum("cdjk,drkb->crjb", blocks(matrix), vector, precision=precise)


def on_columns(vector, matrix):
    return jnp.einsum("cdjk,drak->craj", blocks(matrix), vector, precision=precise)


def plain(amplitudes, gates):
    layout = amplitudes.shape
    slabs, order = layout[1], layout[4]
    vector = amplitudes.reshape(2, slabs, order, order)
    vector = on_columns(on_rows(vector, gates[0, 0]), gates[0, 1])
    vector = lax.all_to_all(vector.reshape(layout), "wide", split_axis=4, concat_axis=2, tiled=True)
    vector = vector.reshape(2, slabs, order, order)
    vector = on_columns(on_rows(vector, gates[1, 0]), gates[1, 1])
    vector = lax.all_to_all(vector.reshape(layout), "narrow", split_axis=4, concat_axis=3, tiled=True)
    vector = vector.reshape(2, slabs, order, order)
    vector = on_columns(on_rows(vector, gates[2, 0]), gates[2, 1])
    return vector.reshape(layout)


def partner(me, mask, count):
    out, bit = 0, 1
    while bit < count:
        digit = me // bit % 2
        if mask & bit:
            digit = 1 - digit
        out = out + digit * bit
        bit *= 2
    return out


def far_first(count):
    return sorted(range(1, count), key=lambda m: (-bin(m >> 1).count("1"), -m))


def split(value):
    high = value.astype(BF16)
    return high, (value - high.astype(F32)).astype(BF16)


def real_form(matrix):
    re, im = matrix[0], matrix[1]
    return jnp.concatenate(
        [jnp.concatenate([re, -im], axis=1), jnp.concatenate([im, re], axis=1)], axis=0
    )


def kernel(wide, narrow, early, amp, gates, out, x, g, y, yr, z, zr, left, right,
           load_sem, gate_sem, ws_sem, wr_sem, ns_sem, nr_sem, es_sem, er_sem):
    slabs, order = amp.shape[1], amp.shape[2]
    last = slabs - 1
    hw, hn = order // wide, order // narrow
    w, n = lax.axis_index("wide"), lax.axis_index("narrow")
    wide_masks = far_first(wide)
    narrow_masks = list(range(1, narrow))

    barrier = pltpu.get_barrier_semaphore()
    for mask in wide_masks:
        pl.semaphore_signal(barrier, inc=1, device_id=(partner(w, mask, wide), n), device_id_type=MESH)
    for mask in narrow_masks:
        pl.semaphore_signal(barrier, inc=1, device_id=(w, partner(n, mask, narrow)), device_id_type=MESH)

    def load(c):
        return pltpu.make_async_copy(amp.at[:, c], x.at[:, c], load_sem.at[c])

    def load_gate(t, k):
        return pltpu.make_async_copy(gates.at[t, k], g.at[t, k], gate_sem.at[t, k])

    load_gate(0, 0).start()
    if early:
        load(last).start()
    load(0).start()
    for t in range(3):
        for k in range(2):
            if (t, k) != (0, 0):
                load_gate(t, k).start()
    for c in range(1, last if early else slabs):
        load(c).start()

    def send_wide(c, i):
        there = partner(w, wide_masks[i], wide)
        return pltpu.make_async_remote_copy(
            src_ref=y.at[c, :, pl.ds(pl.multiple_of(there * hw, hw), hw), :],
            dst_ref=yr.at[c, :, pl.ds(pl.multiple_of(w * hw, hw), hw), :],
            send_sem=ws_sem.at[c, i], recv_sem=wr_sem.at[c, i],
            device_id=(there, n), device_id_type=MESH)

    def send_narrow(c, i):
        there = partner(n, narrow_masks[i], narrow)
        return pltpu.make_async_remote_copy(
            src_ref=z.at[c, :, pl.ds(pl.multiple_of(there * hn, hn), hn), :],
            dst_ref=zr.at[c, :, pl.ds(pl.multiple_of(n * hn, hn), hn), :],
            send_sem=ns_sem.at[c, i], recv_sem=nr_sem.at[c, i],
            device_id=(w, there), device_id_type=MESH)

    def send_early():
        return pltpu.make_async_remote_copy(
            src_ref=x.at[:, last], dst_ref=x.at[:, slabs],
            send_sem=es_sem.at[0], recv_sem=er_sem.at[0],
            device_id=(w, partner(n, 3, narrow)), device_id_type=MESH)

    def send_half(k):
        there = partner(n, 1, narrow)
        index = partner(n, 3 * k, narrow)
        return pltpu.make_async_remote_copy(
            src_ref=z.at[last + k, :, pl.ds(pl.multiple_of(there * hn, hn), hn), :],
            dst_ref=zr.at[last, :, pl.ds(pl.multiple_of(index * hn, hn), hn), :],
            send_sem=es_sem.at[1 + k], recv_sem=er_sem.at[1 + k],
            device_id=(w, there), device_id_type=MESH)

    def prepare(t):
        load_gate(t, 0).wait()
        high, low = split(real_form(g[t, 0]))
        left[t] = jnp.concatenate([high, low, high], axis=1)

    def rows(t, value):
        high, low = split(value.reshape(2 * order, order))
        stacked = jnp.concatenate([high, high, low], axis=0)
        return jnp.dot(left[t], stacked, preferred_element_type=F32)

    def columns(value):
        high, low = split(jnp.concatenate([value[:order], value[order:]], axis=1))
        stacked = jnp.concatenate([high, low, high], axis=1)
        return jnp.dot(stacked, right[...], preferred_element_type=F32)

    def first(c, loaded=False):
        if not loaded:
            load(c).wait()
        y[c] = rows(0, x[:, c]).reshape(2, order, order)

    def start_wide(c):
        for i in range(wide - 1):
            send_wide(c, i).start()

    prepare(0)
    first(0)
    if early:
        load(last).wait()
    pl.semaphore_wait(barrier, wide + narrow - 2)
    if early:
        send_early().start()
    start_wide(0)
    prepare(1)

    @pl.loop(1, last if early else slabs)
    def _(c):
        first(c)
        start_wide(c)

    if early:
        first(last, True)
        start_wide(last)

    def second(c, with_columns, with_narrow=True):
        own = pl.ds(pl.multiple_of(w * hw, hw), hw)
        yr[c, :, own, :] = y[c, :, own, :]
        for i in range(wide - 1):
            send_wide(c, i).wait_recv()
        value = rows(1, yr[c])
        if with_columns:
            value = columns(value)
            z[c, 0] = value[:, :order]
            z[c, 1] = value[:, order:]
        else:
            z[c] = value.reshape(2, order, order)
        if not with_narrow:
            return
        for i in range(narrow - 1):
            send_narrow(c, i).start()

    second(0, False)

    for t in range(3):
        load_gate(t, 1).wait()
    product = g[0, 1].reshape(2 * order, order)
    for t in (1, 2):
        product = jnp.dot(real_form(g[t, 1]), product, precision=precise, preferred_element_type=F32)
    re, im = product[:order].T, product[order:].T
    high, low = split(jnp.concatenate(
        [jnp.concatenate([re, im], axis=1), jnp.concatenate([-im, re], axis=1)], axis=0))
    right[...] = jnp.concatenate([high, high, low], axis=0)
    prepare(2)

    if early:
        @pl.loop(1, EARLY_AT)
        def _(c):
            second(c, True)

        send_early().wait_recv()
        first(slabs, True)
        start_wide(slabs)

        @pl.loop(EARLY_AT, last - TAIL)
        def _(c):
            second(c, True)

        @pl.loop(last, slabs + 1)
        def _(c):
            second(c, False, False)

        for k in range(2):
            send_half(k).start()
            index = partner(n, 3 * k, narrow)
            rows_to = pl.ds(pl.multiple_of(index * hn, hn), hn)
            rows_from = pl.ds(pl.multiple_of(n * hn, hn), hn)
            zr[last, :, rows_to, :] = z[last + k, :, rows_from, :]

        @pl.loop(last - TAIL, last)
        def _(c):
            second(c, True)
    else:
        @pl.loop(1, slabs)
        def _(c):
            second(c, True)

    def third(c, with_columns, exchanged=False):
        if not exchanged:
            own = pl.ds(pl.multiple_of(n * hn, hn), hn)
            zr[c, :, own, :] = z[c, :, own, :]
            for i in range(narrow - 1):
                send_narrow(c, i).wait_recv()
        value = rows(2, zr[c])
        if with_columns:
            value = columns(value)
            out[0, c] = value[:, :order]
            out[1, c] = value[:, order:]
        else:
            out[0, c] = value[:order]
            out[1, c] = value[order:]

    third(0, True)
    if early:
        @pl.loop(1, last - TAIL)
        def _(c):
            third(c, False)

        for k in range(2):
            send_half(k).wait_recv()
        third(last, True, True)

        @pl.loop(last - TAIL, last)
        def _(c):
            third(c, False)
    else:
        @pl.loop(1, slabs)
        def _(c):
            third(c, False)

    @pl.loop(0, slabs + 1 if early else slabs)
    def _(c):
        for i in range(wide - 1):
            send_wide(c, i).wait_send()

    @pl.loop(0, last if early else slabs)
    def _(c):
        for i in range(narrow - 1):
            send_narrow(c, i).wait_send()

    if early:
        send_early().wait_send()
        for k in range(2):
            send_half(k).wait_send()


def fused(wide, narrow, amplitudes, gates):
    layout = amplitudes.shape
    slabs, order = layout[1], layout[4]
    vector = amplitudes.reshape(2, slabs, order, order)
    early = narrow == 4 and slabs > EARLY_AT + TAIL
    slots = slabs + early
    slab_buffer = pltpu.VMEM((slots, 2, order, order), F32)
    result = pl.pallas_call(
        functools.partial(kernel, wide, narrow, early),
        out_shape=jax.ShapeDtypeStruct(vector.shape, F32),
        in_specs=[pl.BlockSpec(memory_space=pl.ANY)] * 2,
        out_specs=pl.BlockSpec(memory_space=pltpu.VMEM),
        scratch_shapes=[
            pltpu.VMEM((2, slots, order, order), F32),
            pltpu.VMEM(gates.shape, F32),
            slab_buffer, slab_buffer, slab_buffer, slab_buffer,
            pltpu.VMEM((3, 2 * order, 6 * order), BF16),
            pltpu.VMEM((6 * order, 2 * order), BF16),
            pltpu.SemaphoreType.DMA((slabs,)),
            pltpu.SemaphoreType.DMA((3, 2)),
            pltpu.SemaphoreType.DMA((slots, wide - 1)),
            pltpu.SemaphoreType.DMA((slots, wide - 1)),
            pltpu.SemaphoreType.DMA((slabs, narrow - 1)),
            pltpu.SemaphoreType.DMA((slabs, narrow - 1)),
            pltpu.SemaphoreType.DMA((3,)),
            pltpu.SemaphoreType.DMA((3,)),
        ],
        compiler_params=pltpu.CompilerParams(
            collective_id=0, has_side_effects=True, vmem_limit_bytes=24 << 20),
    )(*[pltpu.with_memory_space_constraint(value, pltpu.HBM) for value in (vector, gates)])
    return result.reshape(layout)


def tiled(order, count):
    return count > 1 and count & (count - 1) == 0 and order % (8 * count) == 0


def solution(mesh):
    wide, narrow = mesh.shape["wide"], mesh.shape["narrow"]

    def shards(amplitudes, gates):
        order = amplitudes.shape[4]
        if tiled(order, wide) and tiled(order, narrow) and wide * narrow <= 128:
            return fused(wide, narrow, amplitudes, gates)
        return plain(amplitudes, gates)

    return jax.shard_map(
        shards,
        mesh=mesh,
        in_specs=(P(None, None, "wide", "narrow", None, None), P()),
        out_specs=P(None, None, "wide", "narrow", None, None),
        check_vma=False,
    )
```

profile of v0, /device:TPU:0, one launch (start us, length us, event | category | flops | bytes accessed | tf_op | source)
XLA Modules:
  0.0 35.6 jit_solution(15201525353279616078)
XLA Ops:
  0.0 34.6 %shard_map.28 = f32[2,8,128,128]{3,2,1,0:T(8,128)S(1)} custom-call(f32[2,8,128,128]{3,2,1,0:T(8,128)} %bitcast.5, f32[3,2,2,128,128]{4,3,2,1,0:T(8,128)} %gates.1), custom_call_target="tpu_custom_call" | custom-call | tf_op jit(solution)/shard_map/pallas_call | solution.py:295
  34.6 1.0 %copy.5 = f32[2,8,1,1,128,128]{5,4,3,2,1,0:T(8,128)} copy(f32[2,8,1,1,128,128]{5,4,3,2,1,0:T(8,128)S(1)} %bitcast.4) | data formatting | bytes 2097152
where the time goes:
time: 35.7 us; the launch traced here: 35.6 us
  Pallas kernels  34.6 us (97%)
  local copies, waits for them, and re-layouts  0.97 us (3%)
    pallas_call x1, Pallas kernels, fused(): pl.pallas_call(functools.partial(kernel, wide, narrow, early), out_shape=...  34.6 us
    unnamed x1, local copies, waits for them, and re-layouts  0.97 us

commit v1 on v0

--- a/solution.py
+++ b/solution.py
@@ -105,7 +105,7 @@
         return pltpu.make_async_remote_copy(
             src_ref=y.at[c, :, pl.ds(pl.multiple_of(there * hw, hw), hw), :],
             dst_ref=yr.at[c, :, pl.ds(pl.multiple_of(w * hw, hw), hw), :],
-            send_sem=ws_sem.at[c, i], recv_sem=wr_sem.at[c, i],
+            send_sem=ws_sem.at[0], recv_sem=wr_sem.at[c],
             device_id=(there, n), device_id_type=MESH)
 
     def send_narrow(c, i):
@@ -113,7 +113,7 @@
         return pltpu.make_async_remote_copy(
             src_ref=z.at[c, :, pl.ds(pl.multiple_of(there * hn, hn), hn), :],
             dst_ref=zr.at[c, :, pl.ds(pl.multiple_of(n * hn, hn), hn), :],
-            send_sem=ns_sem.at[c, i], recv_sem=nr_sem.at[c, i],
+            send_sem=ns_sem.at[0], recv_sem=nr_sem.at[c],
             device_id=(w, there), device_id_type=MESH)
 
     def send_early():
@@ -131,6 +131,9 @@
             send_sem=es_sem.at[1 + k], recv_sem=er_sem.at[1 + k],
             device_id=(w, there), device_id_type=MESH)
 
+    def arrived(ref, sem):
+        pltpu.make_async_copy(ref, ref, sem).wait()
+
     def prepare(t):
         load_gate(t, 0).wait()
         high, low = split(real_form(g[t, 0]))
@@ -177,8 +180,7 @@
     def second(c, with_columns, with_narrow=True):
         own = pl.ds(pl.multiple_of(w * hw, hw), hw)
         yr[c, :, own, :] = y[c, :, own, :]
-        for i in range(wide - 1):
-            send_wide(c, i).wait_recv()
+        arrived(yr.at[c, :, pl.ds(0, hw * (wide - 1)), :], wr_sem.at[c])
         value = rows(1, yr[c])
         if with_columns:
             value = columns(value)
@@ -240,8 +242,7 @@
         if not exchanged:
             own = pl.ds(pl.multiple_of(n * hn, hn), hn)
             zr[c, :, own, :] = z[c, :, own, :]
-            for i in range(narrow - 1):
-                send_narrow(c, i).wait_recv()
+            arrived(zr.at[c, :, pl.ds(0, hn * (narrow - 1)), :], nr_sem.at[c])
         value = rows(2, zr[c])
         if with_columns:
             value = columns(value)
@@ -269,15 +270,9 @@
         def _(c):
             third(c, False)
 
-    @pl.loop(0, slabs + 1 if early else slabs)
-    def _(c):
-        for i in range(wide - 1):
-            send_wide(c, i).wait_send()
-
-    @pl.loop(0, last if early else slabs)
-    def _(c):
-        for i in range(narrow - 1):
-            send_narrow(c, i).wait_send()
+    arrived(y.at[:, :, pl.ds(0, hw * (wide - 1)), :], ws_sem.at[0])
+    sent = z.at[pl.ds(0, last if early else slabs), :, pl.ds(0, hn * (narrow - 1)), :]
+    arrived(sent, ns_sem.at[0])
 
     if early:
         send_early().wait_send()
@@ -305,10 +300,10 @@
             pltpu.VMEM((6 * order, 2 * order), BF16),
             pltpu.SemaphoreType.DMA((slabs,)),
             pltpu.SemaphoreType.DMA((3, 2)),
-            pltpu.SemaphoreType.DMA((slots, wide - 1)),
-            pltpu.SemaphoreType.DMA((slots, wide - 1)),
-            pltpu.SemaphoreType.DMA((slabs, narrow - 1)),
-            pltpu.SemaphoreType.DMA((slabs, narrow - 1)),
+            pltpu.SemaphoreType.DMA((1,)),
+            pltpu.SemaphoreType.DMA((slots,)),
+            pltpu.SemaphoreType.DMA((1,)),
+            pltpu.SemaphoreType.DMA((slabs,)),
             pltpu.SemaphoreType.DMA((3,)),
             pltpu.SemaphoreType.DMA((3,)),
         ],

time: 35.7 us -> 34.2 us (0.958)
  Pallas kernels: 34.6 us -> 33 us
    pallas_call x1, Pallas kernels: 34.6 us -> 33 us  [fused(): pl.pallas_call(functools.partial(kernel, wide, narrow, early), out_shape=...]
where the time goes in v1:
time: 34.2 us; the launch traced here: 34 us
  Pallas kernels  33 us (96%)
  local copies, waits for them, and re-layouts  0.97 us (3%)
    pallas_call x1, Pallas kernels, fused(): pl.pallas_call(functools.partial(kernel, wide, narrow, early), out_shape=...  33 us
    unnamed x1, local copies, waits for them, and re-layouts  0.97 us

profile of v1, /device:TPU:0, one launch (start us, length us, event | category | flops | bytes accessed | tf_op | source)
XLA Modules:
  0.0 34.0 jit_solution(4070398507417027078)
XLA Ops:
  0.0 33.0 %shard_map.28 = f32[2,8,128,128]{3,2,1,0:T(8,128)S(1)} custom-call(f32[2,8,128,128]{3,2,1,0:T(8,128)} %bitcast.5, f32[3,2,2,128,128]{4,3,2,1,0:T(8,128)} %gates.1), custom_call_target="tpu_custom_call" | custom-call | tf_op jit(solution)/shard_map/pallas_call | solution.py:290
  33.0 1.0 %copy.5 = f32[2,8,1,1,128,128]{5,4,3,2,1,0:T(8,128)} copy(f32[2,8,1,1,128,128]{5,4,3,2,1,0:T(8,128)S(1)} %bitcast.4) | data formatting | bytes 2097152

commit v2 on v1

--- a/solution.py
+++ b/solution.py
@@ -11,7 +11,9 @@
 MESH = pl.DeviceIdType.MESH
 F32 = jnp.float32
 BF16 = jnp.bfloat16
-EARLY_AT = 4
+EARLY_AT = 5
+DEFER = (0, 1)
+DEFER_AT = 3
 TAIL = 1
 
 
@@ -69,7 +71,7 @@
 
 
 def kernel(wide, narrow, early, amp, gates, out, x, g, y, yr, z, zr, left, right,
-           load_sem, gate_sem, ws_sem, wr_sem, ns_sem, nr_sem, es_sem, er_sem):
+           met, load_sem, gate_sem, ws_sem, wr_sem, ns_sem, nr_sem, es_sem, er_sem):
     slabs, order = amp.shape[1], amp.shape[2]
     last = slabs - 1
     hw, hn = order // wide, order // narrow
@@ -77,8 +79,13 @@
     wide_masks = far_first(wide)
     narrow_masks = list(range(1, narrow))
 
+    near = [i for i, mask in enumerate(wide_masks) if bin(mask >> 1).count("1") < 2]
+    distant = [i for i in range(wide - 1) if i not in near]
+    relayed = wide == 8
+    greeted = near if relayed else list(range(wide - 1))
+
     barrier = pltpu.get_barrier_semaphore()
-    for mask in wide_masks:
+    for mask in [wide_masks[i] for i in greeted]:
         pl.semaphore_signal(barrier, inc=1, device_id=(partner(w, mask, wide), n), device_id_type=MESH)
     for mask in narrow_masks:
         pl.semaphore_signal(barrier, inc=1, device_id=(w, partner(n, mask, narrow)), device_id_type=MESH)
@@ -110,6 +117,8 @@
 
     def send_narrow(c, i):
         there = partner(n, narrow_masks[i], narrow)
+        if narrow == 4:
+            there = [partner(n, 1, narrow), 3 - 3 * (n // 2), 2 - n // 2][i]
         return pltpu.make_async_remote_copy(
             src_ref=z.at[c, :, pl.ds(pl.multiple_of(there * hn, hn), hn), :],
             dst_ref=zr.at[c, :, pl.ds(pl.multiple_of(n * hn, hn), hn), :],
@@ -154,21 +163,33 @@
             load(c).wait()
         y[c] = rows(0, x[:, c]).reshape(2, order, order)
 
-    def start_wide(c):
-        for i in range(wide - 1):
+    def start_wide(c, some=None):
+        for i in range(wide - 1) if some is None else some:
             send_wide(c, i).start()
+
+    def meet():
+        pl.semaphore_wait(barrier, len(greeted) + narrow - 1)
+        if relayed:
+            pl.semaphore_signal(met, inc=1, device_id=(partner(w, 2, wide), n), device_id_type=MESH)
+
+    def meet_distant():
+        if relayed:
+            pl.semaphore_wait(met, 1)
 
     prepare(0)
     first(0)
     if early:
         load(last).wait()
-    pl.semaphore_wait(barrier, wide + narrow - 2)
+    meet()
     if early:
         send_early().start()
-    start_wide(0)
-    prepare(1)
-
-    @pl.loop(1, last if early else slabs)
+    start_wide(0, near)
+    first(1)
+    meet_distant()
+    start_wide(0, distant)
+    start_wide(1)
+
+    @pl.loop(2, last if early else slabs)
     def _(c):
         first(c)
         start_wide(c)
@@ -177,7 +198,7 @@
         first(last, True)
         start_wide(last)
 
-    def second(c, with_columns, with_narrow=True):
+    def second(c, with_columns, with_narrow=None):
         own = pl.ds(pl.multiple_of(w * hw, hw), hw)
         yr[c, :, own, :] = y[c, :, own, :]
         arrived(yr.at[c, :, pl.ds(0, hw * (wide - 1)), :], wr_sem.at[c])
@@ -188,13 +209,10 @@
             z[c, 1] = value[:, order:]
         else:
             z[c] = value.reshape(2, order, order)
-        if not with_narrow:
-            return
-        for i in range(narrow - 1):
+        for i in range(narrow - 1) if with_narrow is None else with_narrow:
             send_narrow(c, i).start()
 
-    second(0, False)
-
+    prepare(1)
     for t in range(3):
         load_gate(t, 1).wait()
     product = g[0, 1].reshape(2 * order, order)
@@ -206,10 +224,16 @@
     right[...] = jnp.concatenate([high, high, low], axis=0)
     prepare(2)
 
-    if early:
-        @pl.loop(1, EARLY_AT)
+    second(0, False)
+
+    if early:
+        @pl.loop(1, DEFER_AT)
         def _(c):
             second(c, True)
+
+        @pl.loop(DEFER_AT, EARLY_AT)
+        def _(c):
+            second(c, True, DEFER)
 
         send_early().wait_recv()
         first(slabs, True)
@@ -217,11 +241,11 @@
 
         @pl.loop(EARLY_AT, last - TAIL)
         def _(c):
-            second(c, True)
+            second(c, True, DEFER)
 
         @pl.loop(last, slabs + 1)
         def _(c):
-            second(c, False, False)
+            second(c, False, [])
 
         for k in range(2):
             send_half(k).start()
@@ -232,7 +256,13 @@
 
         @pl.loop(last - TAIL, last)
         def _(c):
-            second(c, True)
+            second(c, True, DEFER)
+
+        @pl.loop(DEFER_AT, last)
+        def _(c):
+            for i in range(narrow - 1):
+                if i not in DEFER:
+                    send_narrow(c, i).start()
     else:
         @pl.loop(1, slabs)
         def _(c):
@@ -298,6 +328,7 @@
             slab_buffer, slab_buffer, slab_buffer, slab_buffer,
             pltpu.VMEM((3, 2 * order, 6 * order), BF16),
             pltpu.VMEM((6 * order, 2 * order), BF16),
+            pltpu.SemaphoreType.REGULAR,
             pltpu.SemaphoreType.DMA((slabs,)),
             pltpu.SemaphoreType.DMA((3, 2)),
             pltpu.SemaphoreType.DMA((1,)),

time: 34.2 us -> 31.5 us (0.921)
  Pallas kernels: 33 us -> 30.4 us
    pallas_call x1, Pallas kernels: 33 us -> 30.4 us  [fused(): pl.pallas_call(functools.partial(kernel, wide, narrow, early), out_shape=...]
where the time goes in v2:
time: 31.5 us; the launch traced here: 31.4 us
  Pallas kernels  30.4 us (97%)
  local copies, waits for them, and re-layouts  0.97 us (3%)
    pallas_call x1, Pallas kernels, fused(): pl.pallas_call(functools.partial(kernel, wide, narrow, early), out_shape=...  30.4 us
    unnamed x1, local copies, waits for them, and re-layouts  0.97 us

profile of v2, /device:TPU:0, one launch (start us, length us, event | category | flops | bytes accessed | tf_op | source)
XLA Modules:
  0.0 31.4 jit_solution(7818993753601109414)
XLA Ops:
  0.0 30.4 %shard_map.28 = f32[2,8,128,128]{3,2,1,0:T(8,128)S(1)} custom-call(f32[2,8,128,128]{3,2,1,0:T(8,128)} %bitcast.5, f32[3,2,2,128,128]{4,3,2,1,0:T(8,128)} %gates.1), custom_call_target="tpu_custom_call" | custom-call | tf_op jit(solution)/shard_map/pallas_call | solution.py:320
  30.4 1.0 %copy.5 = f32[2,8,1,1,128,128]{5,4,3,2,1,0:T(8,128)} copy(f32[2,8,1,1,128,128]{5,4,3,2,1,0:T(8,128)S(1)} %bitcast.4) | data formatting | bytes 2097152

commit v3 on v2

v3 whole, which is shorter than its diff:
```python
import functools

import jax
import jax.numpy as jnp
from jax import lax
from jax.experimental import pallas as pl
from jax.experimental.pallas import tpu as pltpu
from jax.sharding import PartitionSpec as P

precise = lax.Precision.HIGHEST
MESH = pl.DeviceIdType.MESH
F32 = jnp.float32
BF16 = jnp.bfloat16
EARLY_AT = 5
DEFER_AT = 3


def blocks(matrix):
    return jnp.stack([jnp.stack([matrix[0], -matrix[1]]), jnp.stack([matrix[1], matrix[0]])])


def on_rows(vector, matrix):
    return jnp.einsum("cdjk,drkb->crjb", blocks(matrix), vector, precision=precise)


def on_columns(vector, matrix):
    return jnp.einsum("cdjk,drak->craj", blocks(matrix), vector, precision=precise)


def plain(amplitudes, gates):
    layout = amplitudes.shape
    slabs, order = layout[1], layout[4]
    vector = amplitudes.reshape(2, slabs, order, order)
    vector = on_columns(on_rows(vector, gates[0, 0]), gates[0, 1])
    vector = lax.all_to_all(vector.reshape(layout), "wide", split_axis=4, concat_axis=2, tiled=True)
    vector = vector.reshape(2, slabs, order, order)
    vector = on_columns(on_rows(vector, gates[1, 0]), gates[1, 1])
    vector = lax.all_to_all(vector.reshape(layout), "narrow", split_axis=4, concat_axis=3, tiled=True)
    vector = vector.reshape(2, slabs, order, order)
    vector = on_columns(on_rows(vector, gates[2, 0]), gates[2, 1])
    return vector.reshape(layout)


def partner(me, mask, count):
    out, bit = 0, 1
    while bit < count:
        digit = me // bit % 2
        if mask & bit:
            digit = 1 - digit
        out = out + digit * bit
        bit *= 2
    return out


def far_first(count):
    return sorted(range(1, count), key=lambda m: (-bin(m >> 1).count("1"), -m))


def turn(w, count):
    if count != 8:
        return w
    chip = w // 2
    return 2 * (chip % 2 + chip // 2) + 1 - w % 2


def greeters(w, count):
    if count != 8:
        return w
    level = turn(w, count) // 2
    return level * (level + 1) + 1 - w % 2


def split(value):
    high = value.astype(BF16)
    return high, (value - high.astype(F32)).astype(BF16)


def real_form(matrix):
    re, im = matrix[0], matrix[1]
    return jnp.concatenate(
        [jnp.concatenate([re, -im], axis=1), jnp.concatenate([im, re], axis=1)], axis=0
    )


def kernel(wide, narrow, early, amp, gates, out, zr, left, x, g, y, yr, z, right,
           met, x_sem, g_sem, ws_sem, wr_sem, ns_sem, nr_sem, es_sem, er_sem):
    slabs, order = amp.shape[1], amp.shape[2]
    last = slabs - 1
    hw, hn = order // wide, order // narrow
    w, n = lax.axis_index("wide"), lax.axis_index("narrow")
    wide_masks = far_first(wide)
    narrow_masks = list(range(1, narrow))

    def wait(ref, sem):
        pltpu.make_async_copy(ref, ref, sem).wait()

    def load(i):
        part = pl.ds(i, 1) if i < 2 else pl.ds(2, slabs - 2)
        return pltpu.make_async_copy(amp.at[:, part], x.at[:, part], x_sem.at[i])

    def load_gate(i):
        part = pl.ds(0, 1) if i == 0 else pl.ds(1, 5)
        return pltpu.make_async_copy(gates.at[part], g.at[part], g_sem.at[i])

    def apart(mask):
        if wide != 8 or mask < 6:
            return False
        return turn(w, wide) // 2 == 1

    def comes_first(there, mask):
        return (turn(there, wide) < turn(w, wide)) & jnp.logical_not(apart(mask))

    def follows(there, mask):
        return (turn(there, wide) > turn(w, wide)) & jnp.logical_not(apart(mask))

    def greet(after):
        for mask in wide_masks:
            there = partner(w, mask, wide)

            @pl.when(comes_first(there, mask) if not after else follows(there, mask))
            def _():
                sem = pltpu.get_barrier_semaphore() if after else met.at[mask - 1]
                pl.semaphore_signal(sem, inc=1, device_id=(there, n), device_id_type=MESH)
        for mask in narrow_masks:
            there = partner(n, mask, narrow)

            @pl.when((there > n) == after)
            def _():
                sem = pltpu.get_barrier_semaphore() if after else met.at[wide + mask - 2]
                pl.semaphore_signal(sem, inc=1, device_id=(w, there), device_id_type=MESH)

    def send_wide(c, i):
        there = partner(w, wide_masks[i], wide)
        return pltpu.make_async_remote_copy(
            src_ref=y.at[c, :, pl.ds(pl.multiple_of(there * hw, hw), hw), :],
            dst_ref=yr.at[c, :, pl.ds(pl.multiple_of(w * hw, hw), hw), :],
            send_sem=ws_sem.at[0], recv_sem=wr_sem.at[c],
            device_id=(there, n), device_id_type=MESH)

    def send_narrow(c, i):
        there = partner(n, narrow_masks[i], narrow)
        if narrow == 4:
            there = [partner(n, 1, narrow), 3 - 3 * (n // 2), 2 - n // 2][i]
        return pltpu.make_async_remote_copy(
            src_ref=z.at[c, :, pl.ds(pl.multiple_of(there * hn, hn), hn), :],
            dst_ref=zr.at[c, :, pl.ds(pl.multiple_of(n * hn, hn), hn), :],
            send_sem=ns_sem.at[0], recv_sem=nr_sem.at[c],
            device_id=(w, there), device_id_type=MESH)

    def send_early():
        return pltpu.make_async_remote_copy(
            src_ref=amp.at[:, last], dst_ref=x.at[:, slabs],
            send_sem=es_sem.at[0], recv_sem=er_sem.at[0],
            device_id=(w, partner(n, 3, narrow)), device_id_type=MESH)

    def send_half(k):
        there = partner(n, 1, narrow)
        index = partner(n, 3 * k, narrow)
        return pltpu.make_async_remote_copy(
            src_ref=z.at[last + k, :, pl.ds(pl.multiple_of(there * hn, hn), hn), :],
            dst_ref=zr.at[last, :, pl.ds(pl.multiple_of(index * hn, hn), hn), :],
            send_sem=es_sem.at[1], recv_sem=er_sem.at[1],
            device_id=(w, there), device_id_type=MESH)

    def prepare(t):
        high, low = split(real_form(g[2 * t]))
        left[t] = jnp.concatenate([high, low, high], axis=1)

    def rows(t, value):
        high, low = split(value.reshape(2 * order, order))
        stacked = jnp.concatenate([high, high, low], axis=0)
        return jnp.dot(left[t], stacked, preferred_element_type=F32)

    def columns(value):
        high, low = split(jnp.concatenate([value[:order], value[order:]], axis=1))
        stacked = jnp.concatenate([high, low, high], axis=1)
        return jnp.dot(stacked, right[...], preferred_element_type=F32)

    def first(c):
        y[c] = rows(0, x[:, c]).reshape(2, order, order)

    def start_wide_known(c, known):
        for mask in wide_masks if known else wide_masks[::-1]:
            there = partner(w, mask, wide)

            @pl.when(comes_first(there, mask) == known)
            def _():
                if not known:
                    @pl.when(follows(there, mask))
                    def _():
                        pl.semaphore_wait(met.at[mask - 1], 1)
                send_wide(c, wide_masks.index(mask)).start()

    def start_wide(c):
        for i in range(wide - 1):
            send_wide(c, i).start()

    def second(c, with_columns, to):
        own = pl.ds(pl.multiple_of(w * hw, hw), hw)
        yr[c, :, own, :] = y[c, :, own, :]
        wait(yr.at[c, :, pl.ds(0, hw * (wide - 1)), :], wr_sem.at[c])
        value = rows(1, yr[c])
        if with_columns:
            value = columns(value)
            z[c, 0] = value[:, :order]
            z[c, 1] = value[:, order:]
        else:
            z[c] = value.reshape(2, order, order)
        for i in to:
            send_narrow(c, i).start()

    def exchanged(c):
        own = pl.ds(pl.multiple_of(n * hn, hn), hn)
        zr[c, :, own, :] = z[c, :, own, :]
        wait(zr.at[c, :, pl.ds(0, hn * (narrow - 1)), :], nr_sem.at[c])

    def third(c, with_columns, whole=False):
        if not whole:
            exchanged(c)
        value = rows(2, zr[c])
        if with_columns:
            value = columns(value)
            out[0, c] = value[:, :order]
            out[1, c] = value[:, order:]
        else:
            out[0, c] = value[:order]
            out[1, c] = value[order:]

    load_gate(0).start()
    load(0).start()
    greet(True)
    load(1).start()
    load_gate(1).start()
    load(2).start()
    expected = greeters(w, wide) + n

    @pl.when(expected > 0)
    def _():
        pl.semaphore_wait(pltpu.get_barrier_semaphore(), expected)
    if early:
        @pl.when(n >= 2)
        def _():
            send_early().start()
    greet(False)

    load_gate(0).wait()
    prepare(0)
    load(0).wait()
    first(0)
    start_wide_known(0, True)
    if early:
        @pl.when(n == 1)
        def _():
            pl.semaphore_wait(met.at[wide + 1], 1)
            send_early().start()
    start_wide_known(0, False)
    load(1).wait()
    first(1)
    start_wide(1)
    if early:
        @pl.when(n == 0)
        def _():
            pl.semaphore_wait(met.at[wide + 1], 1)
            send_early().start()
    load(2).wait()

    @pl.loop(2, slabs)
    def _(c):
        first(c)
        start_wide(c)

    load_gate(1).wait()
    product = g[1].reshape(2 * order, order)
    for t in (1, 2):
        product = jnp.dot(real_form(g[2 * t + 1]), product, precision=precise, preferred_element_type=F32)
    re, im = product[:order].T, product[order:].T
    high, low = split(jnp.concatenate(
        [jnp.concatenate([re, im], axis=1), jnp.concatenate([-im, re], axis=1)], axis=0))
    right[...] = jnp.concatenate([high, high, low], axis=0)
    prepare(1)
    prepare(2)
    for mask in narrow_masks:
        if not (early and mask == 3):
            @pl.when(partner(n, mask, narrow) > n)
            def _():
                pl.semaphore_wait(met.at[wide + mask - 2], 1)

    everywhere = list(range(narrow - 1))
    if early:
        soon, later = everywhere[:-1], everywhere[-1:]
        second(0, False, everywhere)

        @pl.loop(1, DEFER_AT)
        def _(c):
            second(c, True, everywhere)

        @pl.loop(DEFER_AT, EARLY_AT)
        def _(c):
            second(c, True, soon)

        send_early().wait_recv()
        first(slabs)
        start_wide(slabs)

        @pl.loop(EARLY_AT, last - 1)
        def _(c):
            second(c, True, soon)

        @pl.loop(last, slabs + 1)
        def _(c):
            second(c, False, [])

        for k in range(2):
            send_half(k).start()
            index = partner(n, 3 * k, narrow)
            rows_to = pl.ds(pl.multiple_of(index * hn, hn), hn)
            rows_from = pl.ds(pl.multiple_of(n * hn, hn), hn)
            zr[last, :, rows_to, :] = z[last + k, :, rows_from, :]

        second(last - 1, True, soon)

        @pl.loop(DEFER_AT, last)
        def _(c):
            for i in later:
                send_narrow(c, i).start()
    else:
        second(0, False, everywhere)

        @pl.loop(1, slabs)
        def _(c):
            second(c, True, everywhere)

    third(0, True)
    if early:
        @pl.loop(1, last - 1)
        def _(c):
            third(c, False)

        wait(zr.at[last, :, pl.ds(0, 2 * hn), :], er_sem.at[1])
        third(last, True, True)
        exchanged(last - 1)
    else:
        @pl.loop(1, last)
        def _(c):
            third(c, False)

        exchanged(last)

    wait(y.at[:, :, pl.ds(0, hw * (wide - 1)), :], ws_sem.at[0])
    wait(z.at[pl.ds(0, last if early else slabs), :, pl.ds(0, hn * (narrow - 1)), :], ns_sem.at[0])
    if early:
        send_early().wait_send()
        wait(z.at[last, :, pl.ds(0, 2 * hn), :], es_sem.at[1])


def finish(c, done, arrived, left, out, value, sem):
    slabs, order = done.shape[1], done.shape[2]
    others = [i for i in range(slabs) if i != c]

    def write(i):
        return pltpu.make_async_copy(done.at[:, i], out.at[:, i], sem.at[0])

    for i in others:
        write(i).start()
    high, low = split(arrived[c].reshape(2 * order, order))
    stacked = jnp.concatenate([high, high, low], axis=0)
    value[...] = jnp.dot(left[2], stacked, preferred_element_type=F32).reshape(2, order, order)
    write_last = pltpu.make_async_copy(value, out.at[:, c], sem.at[1])
    write_last.start()
    for i in others:
        write(i).wait()
    write_last.wait()


def fused(wide, narrow, amplitudes, gates):
    layout = amplitudes.shape
    slabs, order = layout[1], layout[4]
    vector = amplitudes.reshape(2, slabs, order, order)
    matrices = gates.reshape(6, 2, order, order)
    early = narrow == 4 and slabs == 8
    slots = slabs + early
    slab_buffer = pltpu.VMEM((slots, 2, order, order), F32)
    done, arrived, left = pl.pallas_call(
        functools.partial(kernel, wide, narrow, early),
        out_shape=[
            jax.ShapeDtypeStruct(vector.shape, F32),
            jax.ShapeDtypeStruct((slabs, 2, order, order), F32),
            jax.ShapeDtypeStruct((3, 2 * order, 6 * order), BF16),
        ],
        in_specs=[pl.BlockSpec(memory_space=pl.ANY)] * 2,
        out_specs=[pl.BlockSpec(memory_space=pltpu.VMEM)] * 3,
        scratch_shapes=[
            pltpu.VMEM((2, slots, order, order), F32),
            pltpu.VMEM(matrices.shape, F32),
            slab_buffer, slab_buffer, slab_buffer,
            pltpu.VMEM((6 * order, 2 * order), BF16),
            pltpu.SemaphoreType.REGULAR((wide + narrow - 2,)),
            pltpu.SemaphoreType.DMA((3,)),
            pltpu.SemaphoreType.DMA((2,)),
            pltpu.SemaphoreType.DMA((1,)),
            pltpu.SemaphoreType.DMA((slots,)),
            pltpu.SemaphoreType.DMA((1,)),
            pltpu.SemaphoreType.DMA((slabs - early,)),
            pltpu.SemaphoreType.DMA((2,)),
            pltpu.SemaphoreType.DMA((2,)),
        ],
        compiler_params=pltpu.CompilerParams(
            collective_id=0, has_side_effects=True, vmem_limit_bytes=24 << 20),
    )(*[pltpu.with_memory_space_constraint(value, pltpu.HBM) for value in (vector, matrices)])
    result = pl.pallas_call(
        functools.partial(finish, slabs - 1 - early),
        out_shape=jax.ShapeDtypeStruct(vector.shape, F32),
        in_specs=[pl.BlockSpec(memory_space=pltpu.VMEM)] * 3,
        out_specs=pl.BlockSpec(memory_space=pltpu.HBM),
        scratch_shapes=[
            pltpu.VMEM((2, order, order), F32),
            pltpu.SemaphoreType.DMA((2,)),
        ],
        compiler_params=pltpu.CompilerParams(vmem_limit_bytes=8 << 20),
    )(done, arrived, left)
    return result.reshape(layout)


def tiled(order, count):
    return count > 1 and count & (count - 1) == 0 and order % (8 * count) == 0


def solution(mesh):
    wide, narrow = mesh.shape["wide"], mesh.shape["narrow"]

    def shards(amplitudes, gates):
        order, slabs = amplitudes.shape[4], amplitudes.shape[1]
        if tiled(order, wide) and tiled(order, narrow) and wide * narrow <= 128 and slabs > 2:
            return fused(wide, narrow, amplitudes, gates)
        return plain(amplitudes, gates)

    return jax.shard_map(
        shards,
        mesh=mesh,
        in_specs=(P(None, None, "wide", "narrow", None, None), P()),
        out_specs=P(None, None, "wide", "narrow", None, None),
        check_vma=False,
    )
```

time: 31.5 us -> 30.7 us (0.975)
  local copies, waits for them, and re-layouts: 0.97 us -> 0 us
    pallas_call x1, Pallas kernels: 30.4 us -> 29.4 us  [fused(): pl.pallas_call(functools.partial(kernel, wide, narrow, early), out_shape=...]
    pallas_call x0 -> x1, Pallas kernels: none -> 0.98 us  [fused(): pl.pallas_call(functools.partial(finish, slabs - 1 - early), out_shape=ja...]
    unnamed x1 -> x0, local copies, waits for them, and re-layouts: 0.97 us -> none
where the time goes in v3:
time: 30.7 us; the launch traced here: 30.4 us
  Pallas kernels  30.4 us (99%)
    pallas_call x1, Pallas kernels, fused(): pl.pallas_call(functools.partial(kernel, wide, narrow, early), out_shape=...  29.4 us
    pallas_call x1, Pallas kernels, fused(): pl.pallas_call(functools.partial(finish, slabs - 1 - early), out_shape=ja...  0.98 us

profile of v3, /device:TPU:0, one launch (start us, length us, event | category | flops | bytes accessed | tf_op | source)
XLA Modules:
  0.0 30.4 jit_solution(8668962401382623734)
XLA Ops:
  0.0 29.4 %shard_map.28 = (f32[2,8,128,128]{3,2,1,0:T(8,128)S(1)}, f32[8,2,128,128]{3,2,1,0:T(8,128)S(1)}, bf16[3,256,768]{2,1,0:T(8,128)(2,1)S(1)}) custom-call(f32[2,8,128,128]{3,2,1,0:T(8,128)} %bitcast.5, f32[6,2,128,128]{3,2,1,0:T(8,128)} %bitcast.6), custom_call_target="tpu_custom_call" | custom-call | tf_op jit(solution)/shard_map/pallas_call | solution.py:383
  29.4 1.0 %shard_map.29 = f32[2,8,128,128]{3,2,1,0:T(8,128)} custom-call(f32[2,8,128,128]{3,2,1,0:T(8,128)S(1)} %get-tuple-element.8.done, f32[8,2,128,128]{3,2,1,0:T(8,128)S(1)} %get-tuple-element.9.arrived, bf16[3,256,768]{2,1,0:T(8,128)(2,1)S(1)} %get-tuple-element.10.left), custom_call_target="tpu_custom_call" | custom-call | tf_op jit(solution)/shard_map/pallas_call | solution.py:410

commit v4 on v3

--- a/solution.py
+++ b/solution.py
@@ -13,6 +13,7 @@
 BF16 = jnp.bfloat16
 EARLY_AT = 5
 DEFER_AT = 3
+AHEAD = 4
 
 
 def blocks(matrix):
@@ -113,6 +114,9 @@
     def follows(there, mask):
         return (turn(there, wide) > turn(w, wide)) & jnp.logical_not(apart(mask))
 
+    def hurried(here, there):
+        return (here == 2) & (there == 1) if early else False
+
     def greet(after):
         for mask in wide_masks:
             there = partner(w, mask, wide)
@@ -124,7 +128,7 @@
         for mask in narrow_masks:
             there = partner(n, mask, narrow)
 
-            @pl.when((there > n) == after)
+            @pl.when((there > n) | hurried(n, there) if after else (there < n) & jnp.logical_not(hurried(n, there)))
             def _():
                 sem = pltpu.get_barrier_semaphore() if after else met.at[wide + mask - 2]
                 pl.semaphore_signal(sem, inc=1, device_id=(w, there), device_id_type=MESH)
@@ -179,16 +183,28 @@
     def first(c):
         y[c] = rows(0, x[:, c]).reshape(2, order, order)
 
+    def answered(mask):
+        @pl.when(follows(partner(w, mask, wide), mask))
+        def _():
+            pl.semaphore_wait(met.at[mask - 1], 1)
+
     def start_wide_known(c, known):
+        if not known and wide == 8:
+            @pl.when(apart(6))
+            def _():
+                for mask in wide_masks[::-1]:
+                    answered(mask)
+                for mask in (7, 6):
+                    send_wide(c, wide_masks.index(mask)).start()
         for mask in wide_masks if known else wide_masks[::-1]:
             there = partner(w, mask, wide)
 
-            @pl.when(comes_first(there, mask) == known)
+            @pl.when(comes_first(there, mask) if known else follows(there, mask))
             def _():
                 if not known:
-                    @pl.when(follows(there, mask))
+                    @pl.when(jnp.logical_not(apart(6)))
                     def _():
-                        pl.semaphore_wait(met.at[mask - 1], 1)
+                        answered(mask)
                 send_wide(c, wide_masks.index(mask)).start()
 
     def start_wide(c):
@@ -209,6 +225,17 @@
         for i in to:
             send_narrow(c, i).start()
 
+    def start_ahead(c):
+        if isinstance(c, int):
+            if c + AHEAD < slabs:
+                first(c + AHEAD)
+                start_wide(c + AHEAD)
+        else:
+            @pl.when(c + AHEAD < slabs)
+            def _():
+                first(c + AHEAD)
+                start_wide(c + AHEAD)
+
     def exchanged(c):
         own = pl.ds(pl.multiple_of(n * hn, hn), hn)
         zr[c, :, own, :] = z[c, :, own, :]
@@ -232,30 +259,28 @@
     load(1).start()
     load_gate(1).start()
     load(2).start()
-    expected = greeters(w, wide) + n
-
-    @pl.when(expected > 0)
-    def _():
-        pl.semaphore_wait(pltpu.get_barrier_semaphore(), expected)
-    if early:
-        @pl.when(n >= 2)
+    def meet():
+        expected = greeters(w, wide) + n + jnp.where(n == 1, 1, 0) if early else greeters(w, wide) + n
+        @pl.when(expected > 0)
         def _():
-            send_early().start()
-    greet(False)
-
+            pl.semaphore_wait(pltpu.get_barrier_semaphore(), expected)
+        if early:
+            @pl.when(n > 0)
+            def _():
+                send_early().start()
+        greet(False)
+
+    pl.when(n != 1)(meet) if early else meet()
     load_gate(0).wait()
     prepare(0)
     load(0).wait()
     first(0)
+    if early:
+        pl.when(n == 1)(meet)
     start_wide_known(0, True)
-    if early:
-        @pl.when(n == 1)
-        def _():
-            pl.semaphore_wait(met.at[wide + 1], 1)
-            send_early().start()
-    start_wide_known(0, False)
     load(1).wait()
     first(1)
+    start_wide_known(0, False)
     start_wide(1)
     if early:
         @pl.when(n == 0)
@@ -264,7 +289,7 @@
             send_early().start()
     load(2).wait()
 
-    @pl.loop(2, slabs)
+    @pl.loop(2, AHEAD)
     def _(c):
         first(c)
         start_wide(c)
@@ -279,6 +304,7 @@
     right[...] = jnp.concatenate([high, high, low], axis=0)
     prepare(1)
     prepare(2)
+
     for mask in narrow_masks:
         if not (early and mask == 3):
             @pl.when(partner(n, mask, narrow) > n)
@@ -289,14 +315,17 @@
     if early:
         soon, later = everywhere[:-1], everywhere[-1:]
         second(0, False, everywhere)
+        start_ahead(0)
 
         @pl.loop(1, DEFER_AT)
         def _(c):
             second(c, True, everywhere)
+            start_ahead(c)
 
         @pl.loop(DEFER_AT, EARLY_AT)
         def _(c):
             second(c, True, soon)
+            start_ahead(c)
 
         send_early().wait_recv()
         first(slabs)
@@ -325,10 +354,12 @@
                 send_narrow(c, i).start()
     else:
         second(0, False, everywhere)
+        start_ahead(0)
 
         @pl.loop(1, slabs)
         def _(c):
             second(c, True, everywhere)
+            start_ahead(c)
 
     third(0, True)
     if early:

time: 30.7 us -> 30.4 us (level)
  the two profiles are of different devices: /device:TPU:0 before, /device:TPU:10 now
where the time goes in v4:
time: 30.4 us; the launch traced here: 30.3 us
  Pallas kernels  30.3 us (100%)
    pallas_call x1, Pallas kernels, fused(): pl.pallas_call(functools.partial(kernel, wide, narrow, early), out_shape=...  29.3 us
    pallas_call x1, Pallas kernels, fused(): pl.pallas_call(functools.partial(finish, slabs - 1 - early), out_shape=ja...  0.98 us

profile of v4, /device:TPU:10, one launch (start us, length us, event | category | flops | bytes accessed | tf_op | source)
XLA Modules:
  0.0 30.3 jit_solution(3035142749937112483)
XLA Ops:
  0.0 29.3 %shard_map.28 = (f32[2,8,128,128]{3,2,1,0:T(8,128)S(1)}, f32[8,2,128,128]{3,2,1,0:T(8,128)S(1)}, bf16[3,256,768]{2,1,0:T(8,128)(2,1)S(1)}) custom-call(f32[2,8,128,128]{3,2,1,0:T(8,128)} %bitcast.5, f32[6,2,128,128]{3,2,1,0:T(8,128)} %bitcast.6), custom_call_target="tpu_custom_call" | custom-call | tf_op jit(solution)/shard_map/pallas_call | solution.py:414
  29.3 1.0 %shard_map.29 = f32[2,8,128,128]{3,2,1,0:T(8,128)} custom-call(f32[2,8,128,128]{3,2,1,0:T(8,128)S(1)} %get-tuple-element.8.done, f32[8,2,128,128]{3,2,1,0:T(8,128)S(1)} %get-tuple-element.9.arrived, bf16[3,256,768]{2,1,0:T(8,128)(2,1)S(1)} %get-tuple-element.10.left), custom_call_target="tpu_custom_call" | custom-call | tf_op jit(solution)/shard_map/pallas_call | solution.py:441

commit v5 on v4

--- a/solution.py
+++ b/solution.py
@@ -12,8 +12,8 @@
 F32 = jnp.float32
 BF16 = jnp.bfloat16
 EARLY_AT = 5
-DEFER_AT = 3
-AHEAD = 4
+DEFER_AT = 4
+AHEAD = 3
 
 
 def blocks(matrix):
@@ -96,7 +96,7 @@
         pltpu.make_async_copy(ref, ref, sem).wait()
 
     def load(i):
-        part = pl.ds(i, 1) if i < 2 else pl.ds(2, slabs - 2)
+        part = [pl.ds(0, 1), pl.ds(last, 1), pl.ds(1, slabs - 2)][i]
         return pltpu.make_async_copy(amp.at[:, part], x.at[:, part], x_sem.at[i])
 
     def load_gate(i):
@@ -153,7 +153,7 @@
 
     def send_early():
         return pltpu.make_async_remote_copy(
-            src_ref=amp.at[:, last], dst_ref=x.at[:, slabs],
+            src_ref=x.at[:, last], dst_ref=x.at[:, slabs],
             send_sem=es_sem.at[0], recv_sem=er_sem.at[0],
             device_id=(w, partner(n, 3, narrow)), device_id_type=MESH)
 
@@ -189,23 +189,33 @@
             pl.semaphore_wait(met.at[mask - 1], 1)
 
     def start_wide_known(c, known):
-        if not known and wide == 8:
-            @pl.when(apart(6))
-            def _():
-                for mask in wide_masks[::-1]:
-                    answered(mask)
-                for mask in (7, 6):
+        def send_to(mask, when):
+            @pl.when(when(partner(w, mask, wide), mask))
+            def _():
+                send_wide(c, wide_masks.index(mask)).start()
+
+        def apart_last():
+            for mask in wide_masks[::-1]:
+                answered(mask)
+            for mask in (4, 5, 7, 6, 3, 2, 1):
+                if mask < 6:
+                    send_to(mask, follows)
+                else:
                     send_wide(c, wide_masks.index(mask)).start()
-        for mask in wide_masks if known else wide_masks[::-1]:
-            there = partner(w, mask, wide)
-
-            @pl.when(comes_first(there, mask) if known else follows(there, mask))
-            def _():
-                if not known:
-                    @pl.when(jnp.logical_not(apart(6)))
-                    def _():
-                        answered(mask)
-                send_wide(c, wide_masks.index(mask)).start()
+
+        def as_answered():
+            for mask in wide_masks[::-1]:
+                answered(mask)
+                send_to(mask, follows)
+
+        if known:
+            for mask in wide_masks:
+                send_to(mask, comes_first)
+        elif wide == 8:
+            pl.when(apart(6))(apart_last)
+            pl.when(jnp.logical_not(apart(6)))(as_answered)
+        else:
+            as_answered()
 
     def start_wide(c):
         for i in range(wide - 1):
@@ -253,17 +263,18 @@
             out[0, c] = value[:order]
             out[1, c] = value[order:]
 
+    load(1).start()
     load_gate(0).start()
     load(0).start()
     greet(True)
-    load(1).start()
+    load(2).start()
     load_gate(1).start()
-    load(2).start()
     def meet():
         expected = greeters(w, wide) + n + jnp.where(n == 1, 1, 0) if early else greeters(w, wide) + n
         @pl.when(expected > 0)
         def _():
             pl.semaphore_wait(pltpu.get_barrier_semaphore(), expected)
+        load(1).wait()
         if early:
             @pl.when(n > 0)
             def _():
@@ -278,22 +289,9 @@
     if early:
         pl.when(n == 1)(meet)
     start_wide_known(0, True)
-    load(1).wait()
+    load(2).wait()
     first(1)
     start_wide_known(0, False)
-    start_wide(1)
-    if early:
-        @pl.when(n == 0)
-        def _():
-            pl.semaphore_wait(met.at[wide + 1], 1)
-            send_early().start()
-    load(2).wait()
-
-    @pl.loop(2, AHEAD)
-    def _(c):
-        first(c)
-        start_wide(c)
-
     load_gate(1).wait()
     product = g[1].reshape(2 * order, order)
     for t in (1, 2):
@@ -304,6 +302,16 @@
     right[...] = jnp.concatenate([high, high, low], axis=0)
     prepare(1)
     prepare(2)
+    start_wide(1)
+    if early:
+        @pl.when(n == 0)
+        def _():
+            pl.semaphore_wait(met.at[wide + 1], 1)
+            send_early().start()
+    @pl.loop(2, AHEAD)
+    def _(c):
+        first(c)
+        start_wide(c)
 
     for mask in narrow_masks:
         if not (early and mask == 3):

time: 30.4 us -> 30.3 us (level)
  the two profiles are of different devices: /device:TPU:10 before, /device:TPU:0 now
where the time goes in v5:
time: 30.3 us; the launch traced here: 29.8 us
  Pallas kernels  29.8 us (98%)
    pallas_call x1, Pallas kernels, fused(): pl.pallas_call(functools.partial(kernel, wide, narrow, early), out_shape=...  28.8 us
    pallas_call x1, Pallas kernels, fused(): pl.pallas_call(functools.partial(finish, slabs - 1 - early), out_shape=ja...  0.98 us

profile of v5, /device:TPU:0, one launch (start us, length us, event | category | flops | bytes accessed | tf_op | source)
XLA Modules:
  0.0 29.8 jit_solution(2002198259891781879)
XLA Ops:
  0.0 28.8 %shard_map.28 = (f32[2,8,128,128]{3,2,1,0:T(8,128)S(1)}, f32[8,2,128,128]{3,2,1,0:T(8,128)S(1)}, bf16[3,256,768]{2,1,0:T(8,128)(2,1)S(1)}) custom-call(f32[2,8,128,128]{3,2,1,0:T(8,128)} %bitcast.5, f32[6,2,128,128]{3,2,1,0:T(8,128)} %bitcast.6), custom_call_target="tpu_custom_call" | custom-call | tf_op jit(solution)/shard_map/pallas_call | solution.py:422
  28.8 1.0 %shard_map.29 = f32[2,8,128,128]{3,2,1,0:T(8,128)} custom-call(f32[2,8,128,128]{3,2,1,0:T(8,128)S(1)} %get-tuple-element.8.done, f32[8,2,128,128]{3,2,1,0:T(8,128)S(1)} %get-tuple-element.9.arrived, bf16[3,256,768]{2,1,0:T(8,128)(2,1)S(1)} %get-tuple-element.10.left), custom_call_target="tpu_custom_call" | custom-call | tf_op jit(solution)/shard_map/pallas_call | solution.py:449

commit v6 on v5

--- a/solution.py
+++ b/solution.py
@@ -84,7 +84,7 @@
 
 
 def kernel(wide, narrow, early, amp, gates, out, zr, left, x, g, y, yr, z, right,
-           met, x_sem, g_sem, ws_sem, wr_sem, ns_sem, nr_sem, es_sem, er_sem):
+           met, load_sem, ws_sem, wr_sem, ns_sem, nr_sem, er_sem):
     slabs, order = amp.shape[1], amp.shape[2]
     last = slabs - 1
     hw, hn = order // wide, order // narrow
@@ -97,11 +97,11 @@
 
     def load(i):
         part = [pl.ds(0, 1), pl.ds(last, 1), pl.ds(1, slabs - 2)][i]
-        return pltpu.make_async_copy(amp.at[:, part], x.at[:, part], x_sem.at[i])
+        return pltpu.make_async_copy(amp.at[:, part], x.at[:, part], load_sem.at[i])
 
     def load_gate(i):
         part = pl.ds(0, 1) if i == 0 else pl.ds(1, 5)
-        return pltpu.make_async_copy(gates.at[part], g.at[part], g_sem.at[i])
+        return pltpu.make_async_copy(gates.at[part], g.at[part], load_sem.at[3 * i])
 
     def apart(mask):
         if wide != 8 or mask < 6:
@@ -114,6 +114,12 @@
     def follows(there, mask):
         return (turn(there, wide) > turn(w, wide)) & jnp.logical_not(apart(mask))
 
+    def wide_met(mask):
+        return 2 + max(mask.bit_length() - 2, 0) + (mask >= 6) if wide == 8 else 2
+
+    def narrow_met(mask):
+        return 1 if early and mask == 3 else 0
+
     def hurried(here, there):
         return (here == 2) & (there == 1) if early else False
 
@@ -123,22 +129,25 @@
 
             @pl.when(comes_first(there, mask) if not after else follows(there, mask))
             def _():
-                sem = pltpu.get_barrier_semaphore() if after else met.at[mask - 1]
+                sem = pltpu.get_barrier_semaphore() if after else met.at[wide_met(mask)]
                 pl.semaphore_signal(sem, inc=1, device_id=(there, n), device_id_type=MESH)
         for mask in narrow_masks:
             there = partner(n, mask, narrow)
 
             @pl.when((there > n) | hurried(n, there) if after else (there < n) & jnp.logical_not(hurried(n, there)))
             def _():
-                sem = pltpu.get_barrier_semaphore() if after else met.at[wide + mask - 2]
+                sem = pltpu.get_barrier_semaphore() if after else met.at[narrow_met(mask)]
                 pl.semaphore_signal(sem, inc=1, device_id=(w, there), device_id_type=MESH)
+
+    def wide_slot(c):
+        return c - jnp.where(c == slabs, 1, 0) if early else c
 
     def send_wide(c, i):
         there = partner(w, wide_masks[i], wide)
         return pltpu.make_async_remote_copy(
             src_ref=y.at[c, :, pl.ds(pl.multiple_of(there * hw, hw), hw), :],
             dst_ref=yr.at[c, :, pl.ds(pl.multiple_of(w * hw, hw), hw), :],
-            send_sem=ws_sem.at[0], recv_sem=wr_sem.at[c],
+            send_sem=ws_sem.at[0], recv_sem=wr_sem.at[wide_slot(c)],
             device_id=(there, n), device_id_type=MESH)
 
     def send_narrow(c, i):
@@ -148,13 +157,13 @@
         return pltpu.make_async_remote_copy(
             src_ref=z.at[c, :, pl.ds(pl.multiple_of(there * hn, hn), hn), :],
             dst_ref=zr.at[c, :, pl.ds(pl.multiple_of(n * hn, hn), hn), :],
-            send_sem=ns_sem.at[0], recv_sem=nr_sem.at[c],
+            send_sem=ns_sem.at[0], recv_sem=nr_sem.at[c // 2],
             device_id=(w, there), device_id_type=MESH)
 
     def send_early():
         return pltpu.make_async_remote_copy(
             src_ref=x.at[:, last], dst_ref=x.at[:, slabs],
-            send_sem=es_sem.at[0], recv_sem=er_sem.at[0],
+            send_sem=ns_sem.at[0], recv_sem=er_sem.at[0],
             device_id=(w, partner(n, 3, narrow)), device_id_type=MESH)
 
     def send_half(k):
@@ -163,7 +172,7 @@
         return pltpu.make_async_remote_copy(
             src_ref=z.at[last + k, :, pl.ds(pl.multiple_of(there * hn, hn), hn), :],
             dst_ref=zr.at[last, :, pl.ds(pl.multiple_of(index * hn, hn), hn), :],
-            send_sem=es_sem.at[1], recv_sem=er_sem.at[1],
+            send_sem=ns_sem.at[0], recv_sem=er_sem.at[1],
             device_id=(w, there), device_id_type=MESH)
 
     def prepare(t):
@@ -183,10 +192,12 @@
     def first(c):
         y[c] = rows(0, x[:, c]).reshape(2, order, order)
 
-    def answered(mask):
-        @pl.when(follows(partner(w, mask, wide), mask))
+    def answered(masks):
+        count = sum(jnp.where(follows(partner(w, mask, wide), mask), 1, 0) for mask in masks)
+
+        @pl.when(count > 0)
         def _():
-            pl.semaphore_wait(met.at[mask - 1], 1)
+            pl.semaphore_wait(met.at[wide_met(masks[0])], count)
 
     def start_wide_known(c, known):
         def send_to(mask, when):
@@ -194,9 +205,11 @@
             def _():
                 send_wide(c, wide_masks.index(mask)).start()
 
+        groups = [(1, 2, 3), (4, 5), (6, 7)] if wide == 8 else [wide_masks[::-1]]
+
         def apart_last():
-            for mask in wide_masks[::-1]:
-                answered(mask)
+            for masks in groups:
+                answered(masks)
             for mask in (4, 5, 7, 6, 3, 2, 1):
                 if mask < 6:
                     send_to(mask, follows)
@@ -204,9 +217,10 @@
                     send_wide(c, wide_masks.index(mask)).start()
 
         def as_answered():
-            for mask in wide_masks[::-1]:
-                answered(mask)
-                send_to(mask, follows)
+            for masks in groups:
+                answered(masks)
+                for mask in masks:
+                    send_to(mask, follows)
 
         if known:
             for mask in wide_masks:
@@ -221,10 +235,11 @@
         for i in range(wide - 1):
             send_wide(c, i).start()
 
-    def second(c, with_columns, to):
+    def second(c, with_columns, to, awaited=1):
         own = pl.ds(pl.multiple_of(w * hw, hw), hw)
         yr[c, :, own, :] = y[c, :, own, :]
-        wait(yr.at[c, :, pl.ds(0, hw * (wide - 1)), :], wr_sem.at[c])
+        if awaited:
+            wait(yr.at[pl.ds(c, awaited), :, pl.ds(0, hw * (wide - 1)), :], wr_sem.at[wide_slot(c)])
         value = rows(1, yr[c])
         if with_columns:
             value = columns(value)
@@ -246,14 +261,15 @@
                 first(c + AHEAD)
                 start_wide(c + AHEAD)
 
-    def exchanged(c):
+    def exchanged(c, awaited):
         own = pl.ds(pl.multiple_of(n * hn, hn), hn)
         zr[c, :, own, :] = z[c, :, own, :]
-        wait(zr.at[c, :, pl.ds(0, hn * (narrow - 1)), :], nr_sem.at[c])
-
-    def third(c, with_columns, whole=False):
-        if not whole:
-            exchanged(c)
+        if awaited:
+            wait(zr.at[pl.ds(c, awaited), :, pl.ds(0, hn * (narrow - 1)), :], nr_sem.at[c // 2])
+
+    def third(c, with_columns, awaited=None):
+        if awaited is not None:
+            exchanged(c, awaited)
         value = rows(2, zr[c])
         if with_columns:
             value = columns(value)
@@ -282,9 +298,8 @@
         greet(False)
 
     pl.when(n != 1)(meet) if early else meet()
-    load_gate(0).wait()
+    wait(g.at[pl.ds(0, 2)], load_sem.at[0])
     prepare(0)
-    load(0).wait()
     first(0)
     if early:
         pl.when(n == 1)(meet)
@@ -306,18 +321,19 @@
     if early:
         @pl.when(n == 0)
         def _():
-            pl.semaphore_wait(met.at[wide + 1], 1)
+            pl.semaphore_wait(met.at[1], 1)
             send_early().start()
     @pl.loop(2, AHEAD)
     def _(c):
         first(c)
         start_wide(c)
 
-    for mask in narrow_masks:
-        if not (early and mask == 3):
-            @pl.when(partner(n, mask, narrow) > n)
-            def _():
-                pl.semaphore_wait(met.at[wide + mask - 2], 1)
+    later_ones = [mask for mask in narrow_masks if narrow_met(mask) == 0]
+    count = sum(jnp.where(partner(n, mask, narrow) > n, 1, 0) for mask in later_ones)
+
+    @pl.when(count > 0)
+    def _():
+        pl.semaphore_wait(met.at[0], count)
 
     everywhere = list(range(narrow - 1))
     if early:
@@ -343,9 +359,8 @@
         def _(c):
             second(c, True, soon)
 
-        @pl.loop(last, slabs + 1)
-        def _(c):
-            second(c, False, [])
+        second(last, False, [], 2)
+        second(slabs, False, [], 0)
 
         for k in range(2):
             send_half(k).start()
@@ -369,27 +384,32 @@
             second(c, True, everywhere)
             start_ahead(c)
 
-    third(0, True)
+    def third_last():
+        wait(zr.at[last, :, pl.ds(0, 2 * hn), :], er_sem.at[1])
+        third(last, True)
+
+    third(0, True, 2)
+    third(1, False, 0)
+    middle = (n == 1) | (n == 2)
     if early:
-        @pl.loop(1, last - 1)
-        def _(c):
-            third(c, False)
-
-        wait(zr.at[last, :, pl.ds(0, 2 * hn), :], er_sem.at[1])
-        third(last, True, True)
-        exchanged(last - 1)
+        pl.when(middle)(third_last)
+
+    @pl.loop(1, (slabs - 1) // 2)
+    def _(p):
+        third(2 * p, False, 2)
+        third(2 * p + 1, False, 0)
+
+    if early:
+        pl.when(jnp.logical_not(middle))(third_last)
+    if early:
+        exchanged(last - 1, 1)
     else:
-        @pl.loop(1, last)
-        def _(c):
-            third(c, False)
-
-        exchanged(last)
+        if slabs % 2 == 0:
+            third(last - 1, False, 2)
+        exchanged(last, 1 if slabs % 2 else 0)
 
     wait(y.at[:, :, pl.ds(0, hw * (wide - 1)), :], ws_sem.at[0])
-    wait(z.at[pl.ds(0, last if early else slabs), :, pl.ds(0, hn * (narrow - 1)), :], ns_sem.at[0])
-    if early:
-        send_early().wait_send()
-        wait(z.at[last, :, pl.ds(0, 2 * hn), :], es_sem.at[1])
+    wait(z.at[:, :, pl.ds(0, hn * (narrow - 1)), :], ns_sem.at[0])
 
 
 def finish(c, done, arrived, left, out, value, sem):
@@ -433,15 +453,13 @@
             pltpu.VMEM(matrices.shape, F32),
             slab_buffer, slab_buffer, slab_buffer,
             pltpu.VMEM((6 * order, 2 * order), BF16),
-            pltpu.SemaphoreType.REGULAR((wide + narrow - 2,)),
-            pltpu.SemaphoreType.DMA((3,)),
-            pltpu.SemaphoreType.DMA((2,)),
+            pltpu.SemaphoreType.REGULAR((5,)),
+            pltpu.SemaphoreType.DMA((4,)),
             pltpu.SemaphoreType.DMA((1,)),
-            pltpu.SemaphoreType.DMA((slots,)),
+            pltpu.SemaphoreType.DMA((slabs,)),
             pltpu.SemaphoreType.DMA((1,)),
-            pltpu.SemaphoreType.DMA((slabs - early,)),
-            pltpu.SemaphoreType.DMA((2,)),
-            pltpu.SemaphoreType.DMA((2,)),
+            pltpu.SemaphoreType.DMA(((slabs + 1 - early) // 2,)),
+            pltpu.SemaphoreType.DMA((1 + early,)),
         ],
         compiler_params=pltpu.CompilerParams(
             collective_id=0, has_side_effects=True, vmem_limit_bytes=24 << 20),

time: 30.3 us -> 30 us (0.990)
  no operation moved by 1% of the time
where the time goes in v6:
time: 30 us; the launch traced here: 29.7 us
  Pallas kernels  29.7 us (99%)
    pallas_call x1, Pallas kernels, fused(): pl.pallas_call(functools.partial(kernel, wide, narrow, early), out_shape=...  28.7 us
    pallas_call x1, Pallas kernels, fused(): pl.pallas_call(functools.partial(finish, slabs - 1 - early), out_shape=ja...  0.98 us

profile of v6, /device:TPU:0, one launch (start us, length us, event | category | flops | bytes accessed | tf_op | source)
XLA Modules:
  0.0 29.7 jit_solution(18439871099985385673)
XLA Ops:
  0.0 28.7 %shard_map.28 = (f32[2,8,128,128]{3,2,1,0:T(8,128)S(1)}, f32[8,2,128,128]{3,2,1,0:T(8,128)S(1)}, bf16[3,256,768]{2,1,0:T(8,128)(2,1)S(1)}) custom-call(f32[2,8,128,128]{3,2,1,0:T(8,128)} %bitcast.5, f32[6,2,128,128]{3,2,1,0:T(8,128)} %bitcast.6), custom_call_target="tpu_custom_call" | custom-call | tf_op jit(solution)/shard_map/pallas_call | solution.py:442
  28.7 1.0 %shard_map.29 = f32[2,8,128,128]{3,2,1,0:T(8,128)} custom-call(f32[2,8,128,128]{3,2,1,0:T(8,128)S(1)} %get-tuple-element.8.done, f32[8,2,128,128]{3,2,1,0:T(8,128)S(1)} %get-tuple-element.9.arrived, bf16[3,256,768]{2,1,0:T(8,128)(2,1)S(1)} %get-tuple-element.10.left), custom_call_target="tpu_custom_call" | custom-call | tf_op jit(solution)/shard_map/pallas_call | solution.py:467

commit v7 on v6

--- a/solution.py
+++ b/solution.py
@@ -11,7 +11,7 @@
 MESH = pl.DeviceIdType.MESH
 F32 = jnp.float32
 BF16 = jnp.bfloat16
-EARLY_AT = 5
+EARLY_AT = 4
 DEFER_AT = 4
 AHEAD = 3
 
@@ -142,6 +142,9 @@
     def wide_slot(c):
         return c - jnp.where(c == slabs, 1, 0) if early else c
 
+    def narrow_slot(c):
+        return jnp.where(c < DEFER_AT, c // 2, c - DEFER_AT // 2) if early else c
+
     def send_wide(c, i):
         there = partner(w, wide_masks[i], wide)
         return pltpu.make_async_remote_copy(
@@ -157,7 +160,7 @@
         return pltpu.make_async_remote_copy(
             src_ref=z.at[c, :, pl.ds(pl.multiple_of(there * hn, hn), hn), :],
             dst_ref=zr.at[c, :, pl.ds(pl.multiple_of(n * hn, hn), hn), :],
-            send_sem=ns_sem.at[0], recv_sem=nr_sem.at[c // 2],
+            send_sem=ns_sem.at[0], recv_sem=nr_sem.at[narrow_slot(c)],
             device_id=(w, there), device_id_type=MESH)
 
     def send_early():
@@ -265,7 +268,7 @@
         own = pl.ds(pl.multiple_of(n * hn, hn), hn)
         zr[c, :, own, :] = z[c, :, own, :]
         if awaited:
-            wait(zr.at[pl.ds(c, awaited), :, pl.ds(0, hn * (narrow - 1)), :], nr_sem.at[c // 2])
+            wait(zr.at[pl.ds(c, awaited), :, pl.ds(0, hn * (narrow - 1)), :], nr_sem.at[narrow_slot(c)])
 
     def third(c, with_columns, awaited=None):
         if awaited is not None:
@@ -358,6 +361,7 @@
         @pl.loop(EARLY_AT, last - 1)
         def _(c):
             second(c, True, soon)
+            start_ahead(c)
 
         second(last, False, [], 2)
         second(slabs, False, [], 0)
@@ -388,25 +392,31 @@
         wait(zr.at[last, :, pl.ds(0, 2 * hn), :], er_sem.at[1])
         third(last, True)
 
-    third(0, True, 2)
-    third(1, False, 0)
     middle = (n == 1) | (n == 2)
     if early:
+        third(0, True, 2)
+        third(1, False, 0)
         pl.when(middle)(third_last)
 
-    @pl.loop(1, (slabs - 1) // 2)
-    def _(p):
-        third(2 * p, False, 2)
-        third(2 * p + 1, False, 0)
-
-    if early:
+        @pl.loop(1, DEFER_AT // 2)
+        def _(p):
+            third(2 * p, False, 2)
+            third(2 * p + 1, False, 0)
+
+        @pl.loop(DEFER_AT, last - 1)
+        def _(c):
+            third(c, False, 1)
+
         pl.when(jnp.logical_not(middle))(third_last)
-    if early:
         exchanged(last - 1, 1)
     else:
-        if slabs % 2 == 0:
-            third(last - 1, False, 2)
-        exchanged(last, 1 if slabs % 2 else 0)
+        third(0, True, 1)
+
+        @pl.loop(1, last)
+        def _(c):
+            third(c, False, 1)
+
+        exchanged(last, 1)
 
     wait(y.at[:, :, pl.ds(0, hw * (wide - 1)), :], ws_sem.at[0])
     wait(z.at[:, :, pl.ds(0, hn * (narrow - 1)), :], ns_sem.at[0])
@@ -458,7 +468,7 @@
             pltpu.SemaphoreType.DMA((1,)),
             pltpu.SemaphoreType.DMA((slabs,)),
             pltpu.SemaphoreType.DMA((1,)),
-            pltpu.SemaphoreType.DMA(((slabs + 1 - early) // 2,)),
+            pltpu.SemaphoreType.DMA((slabs - 1 - DEFER_AT // 2 if early else slabs,)),
             pltpu.SemaphoreType.DMA((1 + early,)),
         ],
         compiler_params=pltpu.CompilerParams(

time: 30 us -> 30 us (level)
  no operation moved by 1% of the time
where the time goes in v7:
time: 30 us; the launch traced here: 29.7 us
  Pallas kernels  29.7 us (99%)
    pallas_call x1, Pallas kernels, fused(): pl.pallas_call(functools.partial(kernel, wide, narrow, early), out_shape=...  28.7 us
    pallas_call x1, Pallas kernels, fused(): pl.pallas_call(functools.partial(finish, slabs - 1 - early), out_shape=ja...  0.98 us

profile of v7, /device:TPU:0, one launch (start us, length us, event | category | flops | bytes accessed | tf_op | source)
XLA Modules:
  0.0 29.7 jit_solution(2568986670800605040)
XLA Ops:
  0.0 28.7 %shard_map.28 = (f32[2,8,128,128]{3,2,1,0:T(8,128)S(1)}, f32[8,2,128,128]{3,2,1,0:T(8,128)S(1)}, bf16[3,256,768]{2,1,0:T(8,128)(2,1)S(1)}) custom-call(f32[2,8,128,128]{3,2,1,0:T(8,128)} %bitcast.5, f32[6,2,128,128]{3,2,1,0:T(8,128)} %bitcast.6), custom_call_target="tpu_custom_call" | custom-call | tf_op jit(solution)/shard_map/pallas_call | solution.py:452
  28.7 1.0 %shard_map.29 = f32[2,8,128,128]{3,2,1,0:T(8,128)} custom-call(f32[2,8,128,128]{3,2,1,0:T(8,128)S(1)} %get-tuple-element.8.done, f32[8,2,128,128]{3,2,1,0:T(8,128)S(1)} %get-tuple-element.9.arrived, bf16[3,256,768]{2,1,0:T(8,128)(2,1)S(1)} %get-tuple-element.10.left), custom_call_target="tpu_custom_call" | custom-call | tf_op jit(solution)/shard_map/pallas_call | solution.py:477

commit v8 on v7

--- a/solution.py
+++ b/solution.py
@@ -99,6 +99,9 @@
         part = [pl.ds(0, 1), pl.ds(last, 1), pl.ds(1, slabs - 2)][i]
         return pltpu.make_async_copy(amp.at[:, part], x.at[:, part], load_sem.at[i])
 
+    def load_last(k):
+        return pltpu.make_async_copy(amp.at[k, last], x.at[k, last], load_sem.at[1 + 3 * k])
+
     def load_gate(i):
         part = pl.ds(0, 1) if i == 0 else pl.ds(1, 5)
         return pltpu.make_async_copy(gates.at[part], g.at[part], load_sem.at[3 * i])
@@ -163,9 +166,9 @@
             send_sem=ns_sem.at[0], recv_sem=nr_sem.at[narrow_slot(c)],
             device_id=(w, there), device_id_type=MESH)
 
-    def send_early():
+    def send_early(k):
         return pltpu.make_async_remote_copy(
-            src_ref=x.at[:, last], dst_ref=x.at[:, slabs],
+            src_ref=x.at[k, last], dst_ref=x.at[k, slabs],
             send_sem=ns_sem.at[0], recv_sem=er_sem.at[0],
             device_id=(w, partner(n, 3, narrow)), device_id_type=MESH)
 
@@ -282,7 +285,8 @@
             out[0, c] = value[:order]
             out[1, c] = value[order:]
 
-    load(1).start()
+    for k in range(2):
+        load_last(k).start()
     load_gate(0).start()
     load(0).start()
     greet(True)
@@ -293,11 +297,12 @@
         @pl.when(expected > 0)
         def _():
             pl.semaphore_wait(pltpu.get_barrier_semaphore(), expected)
-        load(1).wait()
-        if early:
-            @pl.when(n > 0)
-            def _():
-                send_early().start()
+        for k in range(2):
+            load_last(k).wait()
+            if early:
+                @pl.when(n > 0)
+                def _():
+                    send_early(k).start()
         greet(False)
 
     pl.when(n != 1)(meet) if early else meet()
@@ -325,7 +330,8 @@
         @pl.when(n == 0)
         def _():
             pl.semaphore_wait(met.at[1], 1)
-            send_early().start()
+            for k in range(2):
+                send_early(k).start()
     @pl.loop(2, AHEAD)
     def _(c):
         first(c)
@@ -354,7 +360,7 @@
             second(c, True, soon)
             start_ahead(c)
 
-        send_early().wait_recv()
+        wait(x.at[:, slabs], er_sem.at[0])
         first(slabs)
         start_wide(slabs)
 
@@ -464,7 +470,7 @@
             slab_buffer, slab_buffer, slab_buffer,
             pltpu.VMEM((6 * order, 2 * order), BF16),
             pltpu.SemaphoreType.REGULAR((5,)),
-            pltpu.SemaphoreType.DMA((4,)),
+            pltpu.SemaphoreType.DMA((5,)),
             pltpu.SemaphoreType.DMA((1,)),
             pltpu.SemaphoreType.DMA((slabs,)),
             pltpu.SemaphoreType.DMA((1,)),

time: 30 us -> 30 us (level)
  no operation moved by 1% of the time
where the time goes in v8:
time: 30 us; the launch traced here: 29.6 us
  Pallas kernels  29.6 us (99%)
    pallas_call x1, Pallas kernels, fused(): pl.pallas_call(functools.partial(kernel, wide, narrow, early), out_shape=...  28.6 us
    pallas_call x1, Pallas kernels, fused(): pl.pallas_call(functools.partial(finish, slabs - 1 - early), out_shape=ja...  0.98 us

profile of v8, /device:TPU:0, one launch (start us, length us, event | category | flops | bytes accessed | tf_op | source)
XLA Modules:
  0.0 29.6 jit_solution(11584066481345239109)
XLA Ops:
  0.0 28.6 %shard_map.28 = (f32[2,8,128,128]{3,2,1,0:T(8,128)S(1)}, f32[8,2,128,128]{3,2,1,0:T(8,128)S(1)}, bf16[3,256,768]{2,1,0:T(8,128)(2,1)S(1)}) custom-call(f32[2,8,128,128]{3,2,1,0:T(8,128)} %bitcast.5, f32[6,2,128,128]{3,2,1,0:T(8,128)} %bitcast.6), custom_call_target="tpu_custom_call" | custom-call | tf_op jit(solution)/shard_map/pallas_call | solution.py:458
  28.6 1.0 %shard_map.29 = f32[2,8,128,128]{3,2,1,0:T(8,128)} custom-call(f32[2,8,128,128]{3,2,1,0:T(8,128)S(1)} %get-tuple-element.8.done, f32[8,2,128,128]{3,2,1,0:T(8,128)S(1)} %get-tuple-element.9.arrived, bf16[3,256,768]{2,1,0:T(8,128)(2,1)S(1)} %get-tuple-element.10.left), custom_call_target="tpu_custom_call" | custom-call | tf_op jit(solution)/shard_map/pallas_call | solution.py:483

commit v9 on v8

--- a/solution.py
+++ b/solution.py
@@ -68,7 +68,7 @@
     if count != 8:
         return w
     level = turn(w, count) // 2
-    return level * (level + 1) + 1 - w % 2
+    return level * (level + 1) // (1 + w % 2) + 1 - w % 2
 
 
 def split(value):
@@ -111,11 +111,17 @@
             return False
         return turn(w, wide) // 2 == 1
 
+    def through_partner(near, far):
+        return (near % 2 == 0) & (far % 2 == 1) & (turn(near, wide) // 2 < turn(far, wide) // 2) if wide == 8 else False
+
     def comes_first(there, mask):
-        return (turn(there, wide) < turn(w, wide)) & jnp.logical_not(apart(mask))
+        return (turn(there, wide) < turn(w, wide)) & jnp.logical_not(apart(mask)) & jnp.logical_not(through_partner(there, w))
 
     def follows(there, mask):
-        return (turn(there, wide) > turn(w, wide)) & jnp.logical_not(apart(mask))
+        return (turn(there, wide) > turn(w, wide)) & jnp.logical_not(apart(mask)) & jnp.logical_not(through_partner(w, there))
+
+    def not_yet(there, mask):
+        return jnp.logical_not(comes_first(there, mask))
 
     def wide_met(mask):
         return 2 + max(mask.bit_length() - 2, 0) + (mask >= 6) if wide == 8 else 2
@@ -218,7 +224,7 @@
                 answered(masks)
             for mask in (4, 5, 7, 6, 3, 2, 1):
                 if mask < 6:
-                    send_to(mask, follows)
+                    send_to(mask, not_yet)
                 else:
                     send_wide(c, wide_masks.index(mask)).start()
 
@@ -226,7 +232,7 @@
             for masks in groups:
                 answered(masks)
                 for mask in masks:
-                    send_to(mask, follows)
+                    send_to(mask, not_yet)
 
         if known:
             for mask in wide_masks:

time: 30 us -> 29.9 us (level)
  no operation moved by 1% of the time
where the time goes in v9:
time: 29.9 us; the launch traced here: 29.6 us
  Pallas kernels  29.6 us (99%)
    pallas_call x1, Pallas kernels, fused(): pl.pallas_call(functools.partial(kernel, wide, narrow, early), out_shape=...  28.6 us
    pallas_call x1, Pallas kernels, fused(): pl.pallas_call(functools.partial(finish, slabs - 1 - early), out_shape=ja...  0.98 us

profile of v9, /device:TPU:0, one launch (start us, length us, event | category | flops | bytes accessed | tf_op | source)
XLA Modules:
  0.0 29.6 jit_solution(11062908288250949652)
XLA Ops:
  0.0 28.6 %shard_map.28 = (f32[2,8,128,128]{3,2,1,0:T(8,128)S(1)}, f32[8,2,128,128]{3,2,1,0:T(8,128)S(1)}, bf16[3,256,768]{2,1,0:T(8,128)(2,1)S(1)}) custom-call(f32[2,8,128,128]{3,2,1,0:T(8,128)} %bitcast.5, f32[6,2,128,128]{3,2,1,0:T(8,128)} %bitcast.6), custom_call_target="tpu_custom_call" | custom-call | tf_op jit(solution)/shard_map/pallas_call | solution.py:464
  28.6 1.0 %shard_map.29 = f32[2,8,128,128]{3,2,1,0:T(8,128)} custom-call(f32[2,8,128,128]{3,2,1,0:T(8,128)S(1)} %get-tuple-element.8.done, f32[8,2,128,128]{3,2,1,0:T(8,128)S(1)} %get-tuple-element.9.arrived, bf16[3,256,768]{2,1,0:T(8,128)(2,1)S(1)} %get-tuple-element.10.left), custom_call_target="tpu_custom_call" | custom-call | tf_op jit(solution)/shard_map/pallas_call | solution.py:489
